TPU v7x, 256 devices: a whole 4x4x8 slice. The times are simulated.
256 devices in a mesh: scen: 4 (over y), sect: 2 (over core), near: 32 (over z, x).
Axes of the slice: x: 4, y: 4, z: 8, core: 2. Of those that a mesh axis runs over, the one named last changes fastest.
Arguments:
- fields: float32 [20, 1024, 128, 128], P('scen', 'near', 'sect'), parts along dimension 0, may hold values from -6 to 6
- down_state: float32 [12, 4096, 1024], P('scen', 'near', 'sect'), parts along dimension 0, may hold values from -6 to 6
- fire_x: int32 [16], P('scen'), parts along dimension 0, may hold values from 0 to 1023
- hrr_index: int32 [16], P('scen'), parts along dimension 0, may hold values from 0 to 31
- hrr_table: float32 [32], replicated, may hold values from 2 to 20
- profile: float32 [128, 128], P('sect'), may hold values from 0.1 to 1
- courant: float32 [3, 1024], P(None, 'sect'), may hold values from 8 to 262144
- wall_loss: float32 [64, 3, 1024], P(None, None, 'sect'), may hold values from 1e-06 to 0.03
- seg_table: int32 [256], P('near'), may hold values from 0 to 63
Outputs:
- near_next: float32 [20, 1024, 128, 128], P('scen', 'near', 'sect'), parts along dimension 0
- down_next: float32 [12, 4096, 1024], P('scen', 'near', 'sect'), parts along dimension 0
There are 4 independent parts, one for each index of `scen`. A program takes and returns all parts, laid end to end along the dimension named above; an argument that names none is the same for every part. Nothing has to cross between parts.
All inputs are finite; a program needn't handle non-finite values.
Results may differ from a plain program's by a relative error of at most 0.0003.
Values sent between devices are 32-bit elements; how exact they have to be, the bound alone decides.
A program may use at most 128 MiB of HBM per device.

v0:
```python
import math

import jax
import jax.numpy as jnp
from jax import lax
from jax.experimental import pallas as pl
from jax.experimental.pallas import tpu as pltpu
from jax.sharding import PartitionSpec as P

MESH = pl.DeviceIdType.MESH

SEG = 16
time_step = 0.1
kappa_along = 0.2
diffusivity_depth = 0.2
buoyancy = 0.5
screening = 0.0003
source_yields = (0.0, 1.0, 0.5, 0.2, -0.3)

XL = 32
NXD = 4
NZD = 8
LENGTH = XL * NXD * NZD

_t = 2.0 + screening
ROOT = (_t - math.sqrt(_t * _t - 4.0)) / 2.0
GAIN = screening / (1.0 / ROOT - ROOT)


def power(n):
    return ROOT**n


ROUND = 1.0 / (1.0 - power(2 * LENGTH + 2))
GROUP = XL * NXD


def pick(values, index):
    chosen = jnp.float32(values[0])
    for i in range(1, len(values)):
        chosen = jnp.where(index == i, jnp.float32(values[i]), chosen)
    return chosen


def from_below_f(z, s):
    return power(GROUP * (z - 1 - s))


def from_below_b(z, s):
    return power(GROUP * (2 * NZD - 2 - z - s))


def from_above_f(z, s):
    return power(GROUP * (z + s) + 2)


def from_above_b(z, s):
    return power(GROUP * (s - z - 1))


def tunnel_kernel(
    fields, down, fire_x, hrr_index, hrr_table, profile, courant, wall, seg,
    near_out, down_out,
    fbuf, ubuf, halo, dbuf, wallbuf, courbuf, profbuf,
    s1, r1, cross, s2, r2, s3, r3, wseg, fac, rate, pre_a, pre_h,
    fx, hi, ht, sg,
    load_sem, ss1, rs1, ssc, rsc, ssh, rsh, ss2, rs2, ss3, rs3,
):
    me = lax.axis_index("near")
    z = me // NXD
    x = lax.rem(me, NXD)
    rows = fbuf.shape[2]
    quarter = rows // NXD
    spec = dbuf.shape[0]
    chunks = dbuf.shape[1]
    per = spec * chunks // NXD

    def remote(src, dst, send, recv, target):
        return pltpu.make_async_remote_copy(
            src_ref=src, dst_ref=dst, send_sem=send, recv_sem=recv,
            device_id={"near": target}, device_id_type=MESH,
        )

    barrier = pltpu.get_barrier_semaphore()

    def greet(target):
        pl.semaphore_signal(barrier, inc=1, device_id={"near": target}, device_id_type=MESH)

    for k in range(1, NXD):
        greet(z * NXD + lax.rem(x + k, NXD))
    for k in range(1, NZD):
        greet(lax.rem(z + k, NZD) * NXD + x)

    @pl.when(z < NZD - 1)
    def _():
        greet((z + 1) * NXD)

    @pl.when(z > 0)
    def _():
        greet((z - 1) * NXD + NXD - 1)

    loads = [
        pltpu.make_async_copy(src, dst, load_sem.at[i])
        for i, (src, dst) in enumerate((
            (fields.at[pl.ds(0, 1)], fbuf.at[pl.ds(0, 1)]),
            (fields.at[pl.ds(1, 1)], fbuf.at[pl.ds(1, 1)]),
            (seg, sg),
            (fire_x, fx),
            (hrr_index, hi),
            (hrr_table, ht),
            (wall, wallbuf),
            (courant, courbuf),
        ) + tuple((down.at[:, :, pl.ds(128 * c, 128)], dbuf.at[:, c]) for c in range(chunks)) + (
            (fields.at[pl.ds(2, 3)], fbuf.at[pl.ds(2, 3)]),
            (profile, profbuf),
        ))
    ]
    for copy in loads:
        copy.start()

    lane = lax.broadcasted_iota(jnp.int32, (rows, 128), 1)
    not_first = lane > 0
    not_last = lane < 127

    def along_height(f):
        return jnp.where(not_first, pltpu.roll(f, 1, 1), 0.0) + jnp.where(not_last, pltpu.roll(f, 127, 1), 0.0)

    half = 0.5 * time_step
    keep = 1.0 - 2.0 * kappa_along - 2.0 * diffusivity_depth

    loads[0].wait()
    loads[1].wait()

    def velocity(k, ahead, behind):
        u = fbuf[0, k]
        star = keep * u + diffusivity_depth * along_height(u) + (time_step * buoyancy) * fbuf[1, k]
        if ahead is not None:
            star = star + ahead * (kappa_along - half * u)
        if behind is not None:
            star = star + behind * (kappa_along + half * u)
        return star

    star = velocity(0, fbuf[0, 1], None)
    ubuf[0] = star
    near_out[0, 0] = star

    def forward(k, carry):
        f, b, weight = carry
        star = velocity(k, fbuf[0, k + 1], fbuf[0, k - 1])
        f = ROOT * f + star
        ubuf[k] = star
        near_out[0, k] = f
        return f, b + weight * star, weight * ROOT

    f, b, weight = lax.fori_loop(1, XL - 1, forward, (star, star, jnp.float32(ROOT)))
    star = velocity(XL - 1, None, fbuf[0, XL - 2])
    f = ROOT * f + star
    ubuf[XL - 1] = star
    near_out[0, XL - 1] = f
    b = b + power(XL - 1) * star
    for q in range(NXD):
        part = slice(q * quarter, (q + 1) * quarter)
        s1[q, 0:quarter] = f[part]
        s1[q, quarter : 2 * quarter] = b[part]
        s1[q, 2 * quarter : 3 * quarter] = fbuf[0, 0, part]
        s1[q, 3 * quarter : 4 * quarter] = fbuf[0, XL - 1, part]

    for copy in loads[2:-2]:
        copy.wait()
    segments = dbuf.shape[2] // SEG
    for s in range(segments):
        for p in range(spec):
            wseg[p, s : s + 1] = wallbuf[p, pl.ds(sg[s], 1)]
    base_a = 4 * quarter
    base_h = base_a + per
    sub = lax.broadcasted_iota(jnp.int32, (segments, 128), 0)
    for r in range(spec * chunks):
        p, c = divmod(r, chunks)
        cols = slice(c * 128, (c + 1) * 128)
        col = courbuf[p : p + 1, cols]
        factor = 1.0 / ((1.0 + col) * (1.0 + wseg[p, :, cols]))
        a = col * factor
        fac[r] = factor
        rate[r] = a
        h = jnp.zeros((segments, 128), jnp.float32)
        for j in range(SEG):
            h = a * h + factor * dbuf[p, c, pl.ds(j, segments, stride=SEG), :]
        for _ in range(4):
            a = a * a
        for shift in (1, 2, 4):
            ok = sub >= shift
            a_prev = jnp.where(ok, pltpu.roll(a, shift, 0), 1.0)
            h_prev = jnp.where(ok, pltpu.roll(h, shift, 0), 0.0)
            h = a * h_prev + h
            a = a * a_prev
        pre_a[r] = jnp.where(sub >= 1, pltpu.roll(a, 1, 0), 1.0)
        pre_h[r] = jnp.where(sub >= 1, pltpu.roll(h, 1, 0), 0.0)
        q, i = divmod(r, per)
        s1[q, base_a + i : base_a + i + 1] = a[segments - 1 : segments]
        s1[q, base_h + i : base_h + i + 1] = h[segments - 1 : segments]
    for q in range(NXD):
        s1[q, base_h + per :] = jnp.zeros((s1.shape[1] - base_h - per, 128), jnp.float32)

    loads[-2].wait()
    loads[-1].wait()
    first_layer = me * XL

    def heat_at(k):
        total = jnp.float32(0.0)
        for i in range(fx.shape[0]):
            total = total + jnp.where(fx[i] == first_layer + k, ht[hi[i]], 0.0)
        return total * time_step

    def transported(i, k, ahead, behind, heat):
        f = fbuf[i, k]
        return (
            keep * f + diffusivity_depth * along_height(f)
            + kappa_along * (ahead + behind) - half * fbuf[0, k] * (ahead - behind)
            + source_yields[i] * heat
        )

    @pl.when(me == NXD * NZD - 1)
    def _():
        heat = heat_at(XL - 1) * profbuf[...]
        from_lane = lax.broadcasted_iota(jnp.int32, (128, 128), 0)
        to_lane = lax.broadcasted_iota(jnp.int32, (128, 128), 1)
        pool = jnp.where(from_lane // 4 == lax.rem(to_lane, 32), 1.0 / 16.0, 0.0)
        row = lax.broadcasted_iota(jnp.int32, (rows, 128), 0)
        kept = lax.rem(row, 16) // 4 == lane // 32
        for p in range(spec):
            layer = transported(p + 1, XL - 1, jnp.zeros((rows, 128), jnp.float32), fbuf[p + 1, XL - 2], heat)
            pooled = jnp.dot(layer, pool, precision=lax.Precision.HIGHEST, preferred_element_type=jnp.float32)
            pooled = jnp.where(kept, pooled, 0.0)
            for c in range(chunks):
                q, i = divmod(p * chunks + c, per)
                s1[q, base_h + i : base_h + i + 1] = jnp.sum(pooled[16 * c : 16 * c + 16], axis=0, keepdims=True)

    r1[x] = s1[x]

    last_z, last_x = NZD - 1, NXD - 1
    extra = 4 * jnp.where((x == 0) & (z > 0), 1, 0) + 4 * jnp.where((x == last_x) & (z < last_z), 1, 0)
    pl.semaphore_wait(barrier, NXD - 1 + NZD - 1 + extra)

    sends = []
    for k in range(1, NXD):
        to = lax.rem(x + k, NXD)
        copy = remote(s1.at[to], r1.at[x], ss1.at[k - 1], rs1.at[x], z * NXD + to)
        copy.start()
        sends.append(copy)

    def crossing(low):
        side = 2 if low else 3
        target = (z - 1 if low else z + 1) * NXD
        return [
            remote(s1.at[q, pl.ds(side * quarter, quarter)], cross.at[1 if low else 0],
                   ssc.at[0 if low else 1, q], rsc.at[1 if low else 0], target + q)
            for q in range(NXD)
        ]

    @pl.when((x == 0) & (z > 0))
    def _():
        for copy in crossing(True):
            copy.start()

    @pl.when((x == last_x) & (z < last_z))
    def _():
        for copy in crossing(False):
            copy.start()

    up = remote(fbuf.at[:, pl.ds(XL - 1, 1)], halo.at[0], ssh.at[0], rsh.at[0], me + 1)
    low = remote(fbuf.at[:, pl.ds(0, 1)], halo.at[1], ssh.at[1], rsh.at[1], me - 1)
    last = NXD * NZD - 1

    @pl.when(me < last)
    def _():
        up.start()

    @pl.when(me > 0)
    def _():
        low.start()

    def inner(k, carry):
        heat = heat_at(k) * profbuf[...]
        for i in range(1, 5):
            near_out[i, k] = transported(i, k, fbuf[i, k + 1], fbuf[i, k - 1], heat)
        return carry

    lax.fori_loop(1, XL - 1, inner, 0)

    def backward(n, b):
        k = XL - 1 - n
        near_out[0, k] = GAIN * (near_out[0, k] + ROOT * b)
        return ubuf[k] + ROOT * b

    lax.fori_loop(0, XL, backward, jnp.zeros((rows, 128), jnp.float32))

    for k in range(1, NXD):
        source = lax.rem(x + k, NXD)
        remote(r1.at[source], r1.at[source], ss1.at[0], rs1.at[source], me).wait_recv()

    @pl.when(z > 0)
    def _():
        remote(cross.at[0], cross.at[0], ssc.at[0, 0], rsc.at[0], me).wait_recv()

    @pl.when(z == 0)
    def _():
        cross[0] = jnp.zeros((quarter, 128), jnp.float32)

    @pl.when(z < last_z)
    def _():
        remote(cross.at[1], cross.at[1], ssc.at[0, 0], rsc.at[1], me).wait_recv()

    @pl.when(z == last_z)
    def _():
        cross[1] = jnp.zeros((quarter, 128), jnp.float32)

    lows = [r1[i, 2 * quarter : 3 * quarter] for i in range(NXD)]
    highs = [r1[i, 3 * quarter : 4 * quarter] for i in range(NXD)]
    sum_f, sum_b = [], []
    for i in range(NXD):
        before = cross[0] if i == 0 else highs[i - 1]
        after = cross[1] if i == NXD - 1 else lows[i + 1]
        at_low = before * (kappa_along + half * lows[i])
        at_high = after * (kappa_along - half * highs[i])
        sum_f.append(r1[i, 0:quarter] + power(XL - 1) * at_low + at_high)
        sum_b.append(r1[i, quarter : 2 * quarter] + at_low + power(XL - 1) * at_high)
    group_f = sum_f[0]
    for i in range(1, NXD):
        group_f = power(XL) * group_f + sum_f[i]
    group_b = sum_b[NXD - 1]
    for i in reversed(range(NXD - 1)):
        group_b = power(XL) * group_b + sum_b[i]
    rates = [r1[i, base_a : base_a + per] for i in range(NXD)]
    drives = [r1[i, base_h : base_h + per] for i in range(NXD)]
    group_a, group_h = rates[0], drives[0]
    for i in range(1, NXD):
        group_a, group_h = rates[i] * group_a, rates[i] * group_h + drives[i]
    pad = jnp.zeros((s2.shape[1] - quarter - 2 * per, 128), jnp.float32)
    s2[0, 0:quarter] = ROUND * (group_f + pick([power(GROUP + 2 + 2 * GROUP * i) for i in range(NZD)], z) * group_b)
    s2[1, 0:quarter] = ROUND * (group_b + pick([power(GROUP * (2 * NZD - 1) - 2 * GROUP * i) for i in range(NZD)], z) * group_f)
    for side in range(2):
        s2[side, quarter : quarter + per] = group_a
        s2[side, quarter + per : quarter + 2 * per] = jnp.where(z == last_z, drives[NXD - 1], group_h)
        s2[side, quarter + 2 * per :] = pad
    for k in range(1, NZD):
        to = lax.rem(z + k, NZD)
        side = jnp.where(to > z, 0, 1)
        copy = remote(s2.at[side], r2.at[z], ss2.at[k - 1], rs2.at[z], to * NXD + x)
        copy.start()
        sends.append(copy)
    r2[z] = s2[0]

    @pl.when(me > 0)
    def _():
        remote(halo.at[0], halo.at[0], ssh.at[0], rsh.at[0], me).wait_recv()

    @pl.when(me == 0)
    def _():
        halo[0] = jnp.zeros(halo.shape[1:], jnp.float32)

    @pl.when(me < last)
    def _():
        remote(halo.at[1], halo.at[1], ssh.at[0], rsh.at[1], me).wait_recv()

    @pl.when(me == last)
    def _():
        halo[1] = jnp.zeros(halo.shape[1:], jnp.float32)

    heat_low = heat_at(0) * profbuf[...]
    heat_high = heat_at(XL - 1) * profbuf[...]
    for i in range(1, 5):
        near_out[i, 0] = transported(i, 0, fbuf[i, 1], halo[0, i, 0], heat_low)
        near_out[i, XL - 1] = transported(i, XL - 1, halo[1, i, 0], fbuf[i, XL - 2], heat_high)

    for k in range(1, NZD):
        source = lax.rem(z + k, NZD)
        remote(r2.at[source], r2.at[source], ss2.at[0], rs2.at[source], me).wait_recv()

    in_f = ROUND * (pick([power(2 * GROUP * i + 2) for i in range(NZD)], z) * group_b + power(2 * LENGTH - GROUP + 2) * group_f)
    in_b = ROUND * (pick([power(2 * GROUP * (NZD - 1 - i)) for i in range(NZD)], z) * group_f + power(2 * LENGTH - GROUP + 2) * group_b)
    for s in range(NZD):
        part = r2[s, 0:quarter]
        coef_f = pick([from_below_f(i, s) if s < i else from_above_f(i, s) if s > i else 0.0 for i in range(NZD)], z)
        coef_b = pick([from_below_b(i, s) if s < i else from_above_b(i, s) if s > i else 0.0 for i in range(NZD)], z)
        in_f = in_f + coef_f * part
        in_b = in_b + coef_b * part
    arrive = r2[NZD - 1, quarter + per : quarter + 2 * per]
    for s in range(NZD - 1):
        passed = r2[s, quarter : quarter + per] * arrive + r2[s, quarter + per : quarter + 2 * per]
        arrive = jnp.where(s < z, passed, arrive)
    f_at = in_f
    for i in range(NXD):
        s3[i, 0:quarter] = f_at
        f_at = power(XL) * f_at + sum_f[i]
        s3[i, 2 * quarter : 2 * quarter + per] = arrive
        arrive = rates[i] * arrive + drives[i]
        s3[i, 2 * quarter + per :] = jnp.zeros((s3.shape[1] - 2 * quarter - per, 128), jnp.float32)
    b_at = in_b
    for i in reversed(range(NXD)):
        s3[i, quarter : 2 * quarter] = b_at
        b_at = power(XL) * b_at + sum_b[i]
    for k in range(1, NXD):
        to = lax.rem(x + k, NXD)
        copy = remote(s3.at[to], r3.at[x], ss3.at[k - 1], rs3.at[x], z * NXD + to)
        copy.start()
        sends.append(copy)
    r3[x] = s3[x]

    for k in range(1, NXD):
        source = lax.rem(x + k, NXD)
        remote(r3.at[source], r3.at[source], ss3.at[0], rs3.at[source], me).wait_recv()

    from_low = jnp.concatenate([r3[q, 0:quarter] for q in range(NXD)], axis=0)
    from_high = jnp.concatenate([r3[q, quarter : 2 * quarter] for q in range(NXD)], axis=0)
    from_low = GAIN * (ROOT * from_low + halo[0, 0, 0] * (kappa_along + half * fbuf[0, 0]))
    from_high = GAIN * (ROOT * from_high + halo[1, 0, 0] * (kappa_along - half * fbuf[0, XL - 1]))
    for k in range(XL):
        near_out[0, k] = near_out[0, k] + (power(k) * from_low + power(XL - 1 - k) * from_high)

    for r in range(spec * chunks):
        p, c = divmod(r, chunks)
        q, i = divmod(r, per)
        a, factor = rate[r], fac[r]
        h = pre_a[r] * r3[q, 2 * quarter + i : 2 * quarter + i + 1] + pre_h[r]
        for j in range(SEG):
            at = pl.ds(j, segments, stride=SEG)
            h = a * h + factor * dbuf[p, c, at, :]
            down_out[p, c, at, :] = h

    for copy in sends:
        copy.wait_send()

    @pl.when((x == 0) & (z > 0))
    def _():
        for copy in crossing(True):
            copy.wait_send()

    @pl.when((x == last_x) & (z < last_z))
    def _():
        for copy in crossing(False):
            copy.wait_send()

    @pl.when(me < last)
    def _():
        up.wait_send()

    @pl.when(me > 0)
    def _():
        low.wait_send()


def write_kernel(near_in, down_in, near_out, down_out, sem):
    copies = [
        pltpu.make_async_copy(near_in.at[i, pl.ds(h * 16, 16)], near_out.at[i, pl.ds(h * 16, 16)], sem.at[2 * i + h])
        for i in range(5) for h in range(2)
    ]
    copies += [
        pltpu.make_async_copy(down_in.at[:, c], down_out.at[:, :, pl.ds(128 * c, 128)], sem.at[10 + c])
        for c in range(down_in.shape[1])
    ]
    for copy in copies:
        copy.start()
    for copy in copies:
        copy.wait()


def body(fields, down_state, fire_x, hrr_index, hrr_table, profile, courant, wall_loss, seg_table):
    f32 = jnp.float32
    rows = fields.shape[2]
    quarter = rows // NXD
    spec, cells, columns = down_state.shape
    segments = cells // SEG
    lines = spec * columns // 128
    per = lines // NXD

    def padded(n):
        return -(-n // 8) * 8

    n1, n2, n3 = padded(4 * quarter + 2 * per), padded(quarter + 2 * per), padded(2 * quarter + per)
    vmem, smem, dma = pltpu.VMEM, pltpu.SMEM, pltpu.SemaphoreType.DMA
    hbm = pl.BlockSpec(memory_space=pltpu.HBM)
    in_vmem = pl.BlockSpec(memory_space=pltpu.VMEM)
    chunked = (spec, columns // 128, cells, 128)
    near_v, down_v = pl.pallas_call(
        tunnel_kernel,
        out_shape=(jax.ShapeDtypeStruct(fields.shape, f32), jax.ShapeDtypeStruct(chunked, f32)),
        in_specs=[hbm] * 9,
        out_specs=(in_vmem, in_vmem),
        scratch_shapes=[
            vmem(fields.shape, f32),
            vmem(fields.shape[1:], f32),
            vmem((2, 5, 1, rows, 128), f32),
            vmem(chunked, f32),
            vmem((spec, wall_loss.shape[0], columns), f32),
            vmem(courant.shape, f32),
            vmem(profile.shape, f32),
            vmem((NXD, n1, 128), f32),
            vmem((NXD, n1, 128), f32),
            vmem((2, quarter, 128), f32),
            vmem((2, n2, 128), f32),
            vmem((NZD, n2, 128), f32),
            vmem((NXD, n3, 128), f32),
            vmem((NXD, n3, 128), f32),
            vmem((spec, segments, columns), f32),
            vmem((lines, segments, 128), f32),
            vmem((lines, segments, 128), f32),
            vmem((lines, segments, 128), f32),
            vmem((lines, segments, 128), f32),
            smem(fire_x.shape, jnp.int32),
            smem(hrr_index.shape, jnp.int32),
            smem(hrr_table.shape, f32),
            smem(seg_table.shape, jnp.int32),
            dma((14,)),
            dma((NXD - 1,)),
            dma((NXD,)),
            dma((2, NXD)),
            dma((2,)),
            dma((2,)),
            dma((2,)),
            dma((NZD - 1,)),
            dma((NZD,)),
            dma((NXD - 1,)),
            dma((NXD,)),
        ],
        compiler_params=pltpu.CompilerParams(
            collective_id=0, has_side_effects=True, vmem_limit_bytes=32 * 1024 * 1024
        ),
        name="tunnel_step",
    )(*(pltpu.with_memory_space_constraint(a, pltpu.HBM) for a in (fields, down_state, fire_x, hrr_index, hrr_table, profile, courant, jnp.transpose(wall_loss, (1, 0, 2)), seg_table)))
    return pl.pallas_call(
        write_kernel,
        out_shape=(jax.ShapeDtypeStruct(fields.shape, f32), jax.ShapeDtypeStruct(down_state.shape, f32)),
        in_specs=[in_vmem, in_vmem],
        out_specs=(hbm, hbm),
        scratch_shapes=[dma((14,))],
        compiler_params=pltpu.CompilerParams(vmem_limit_bytes=16 * 1024 * 1024),
        name="write_out",
    )(near_v, down_v)


def solution(mesh):
    placed = (
        P("scen", "near", "sect", None),
        P("scen", "near", "sect"),
        P("scen"),
        P("scen"),
        P(),
        P("sect", None),
        P(None, "sect"),
        P(None, None, "sect"),
        P("near"),
    )
    return jax.shard_map(
        body,
        mesh=mesh,
        in_specs=placed,
        out_specs=(P("scen", "near", "sect", None), P("scen", "near", "sect")),
        check_vma=False,
    )
```

profile of v0, /device:TPU:8, one launch (start us, length us, event | category | flops | bytes accessed | tf_op | source)
XLA Modules:
  0.0 30.4 jit_solution(14598544422592300994)
XLA Ops:
  0.6 27.1 %tunnel_step.1 = (f32[5,32,64,128]{3,2,1,0:T(8,128)S(1)}, f32[3,4,128,128]{3,2,1,0:T(8,128)S(1)}) custom-call(f32[5,32,64,128]{3,2,1,0:T(8,128)} %fields.1, f32[3,128,512]{2,1,0:T(8,128)} %down.1, s32[4]{0:T(128)} %fire_x.1, s32[4]{0:T(128)} %hrr_index.1, f32[32]{0:T(128)} %hrr_table.1, f32[64,128]{1,0:T(8,128)} %profile.1, f32[3,512]{1,0:T(4,128)} %courant.1, ...), custom_call_target="tpu_custom_call" | custom-call | tf_op jit(solution)/shard_map/tunnel_step/pallas_call | solution.py:484
  27.7 2.7 %write_out.1 = (f32[5,32,64,128]{3,2,1,0:T(8,128)}, f32[3,128,512]{2,1,0:T(8,128)}) custom-call(f32[5,32,64,128]{3,2,1,0:T(8,128)S(1)} %get-tuple-element.4.near_in, f32[3,4,128,128]{3,2,1,0:T(8,128)S(1)} %get-tuple-element.5.down_in), custom_call_target="tpu_custom_call" | custom-call | tf_op jit(solution)/shard_map/write_out/pallas_call | solution.py:530
where the time goes:
time: 30.6 us; the launch traced here: 30.4 us
  Pallas kernels  29.8 us (97%)
  between operations  0.64 us (2%)
    pallas_call x1, Pallas kernels, body(): pl.pallas_call(tunnel_kernel, out_shape=(jax.ShapeDtypeStruct(fields.shap...  27.1 us
    pallas_call x1, Pallas kernels, body(): pl.pallas_call(write_kernel, out_shape=(jax.ShapeDtypeStruct(fields.shape...  2.67 us

commit v1 on v0

v1 whole, which is shorter than its diff:
```python
import math

import jax
import jax.numpy as jnp
from jax import lax
from jax.experimental import pallas as pl
from jax.experimental.pallas import tpu as pltpu
from jax.sharding import PartitionSpec as P

MESH = pl.DeviceIdType.MESH

SEG = 16
time_step = 0.1
kappa_along = 0.2
diffusivity_depth = 0.2
buoyancy = 0.5
screening = 0.0003
source_yields = (0.0, 1.0, 0.5, 0.2, -0.3)

XL = 32
NXD = 4
NZD = 8
LENGTH = XL * NXD * NZD

_t = 2.0 + screening
ROOT = (_t - math.sqrt(_t * _t - 4.0)) / 2.0
GAIN = screening / (1.0 / ROOT - ROOT)


def power(n):
    return ROOT**n


ROUND = 1.0 / (1.0 - power(2 * LENGTH + 2))
GROUP = XL * NXD


def pick(values, index):
    chosen = jnp.float32(values[0])
    for i in range(1, len(values)):
        chosen = jnp.where(index == i, jnp.float32(values[i]), chosen)
    return chosen


def from_below_f(z, s):
    return power(GROUP * (z - 1 - s))


def from_below_b(z, s):
    return power(GROUP * (2 * NZD - 2 - z - s))


def from_above_f(z, s):
    return power(GROUP * (z + s) + 2)


def from_above_b(z, s):
    return power(GROUP * (s - z - 1))


def tunnel_kernel(
    fields, down, fire_x, hrr_index, hrr_table, profile, courant, wall, seg,
    near_out, edges, dbuf, fac, rate, start,
    fbuf, ubuf, halo, tail, wallbuf, courbuf, profbuf,
    se, re, s1, r1, cross, s2, r2, s3, r3, d1, e1, d2, e2, d3, e3, wseg, pre_a, pre_h,
    fx, hi, ht, sg,
    load_sem, sse, rse, ss1, rs1, ssc, rsc, ssh, rsh, ss2, rs2, ss3, rs3, sd1, rd1, sd2, rd2, sd3, rd3,
):
    me = lax.axis_index("near")
    z = me // NXD
    x = lax.rem(me, NXD)
    last, last_z, last_x = NXD * NZD - 1, NZD - 1, NXD - 1
    rows = fbuf.shape[2]
    quarter = rows // NXD
    spec = dbuf.shape[0]
    chunks = dbuf.shape[1]
    per = spec * chunks // NXD
    lines = [divmod(r, chunks) for r in range(spec * chunks)]

    def remote(src, dst, send, recv, target):
        return pltpu.make_async_remote_copy(
            src_ref=src, dst_ref=dst, send_sem=send, recv_sem=recv,
            device_id={"near": target}, device_id_type=MESH,
        )

    barrier = pltpu.get_barrier_semaphore()

    def greet(target):
        pl.semaphore_signal(barrier, inc=1, device_id={"near": target}, device_id_type=MESH)

    for k in range(1, NZD):
        greet(lax.rem(z + k, NZD) * NXD + x)
    for k in range(1, NXD):
        greet(z * NXD + lax.rem(x + k, NXD))

    @pl.when(z < last_z)
    def _():
        greet((z + 1) * NXD)

    @pl.when(z > 0)
    def _():
        greet((z - 1) * NXD + last_x)

    half_layers = XL // 2
    loads = [
        pltpu.make_async_copy(src, dst, load_sem.at[i])
        for i, (src, dst) in enumerate(tuple(
            (fields.at[pl.ds(f, 1), pl.ds(h * half_layers, half_layers)], fbuf.at[pl.ds(f, 1), pl.ds(h * half_layers, half_layers)])
            for h in range(2) for f in range(2)
        ) + (
            (seg, sg),
            (courant, courbuf),
            (wall, wallbuf),
        ) + tuple((down.at[:, :, pl.ds(128 * c, 128)], dbuf.at[:, c]) for c in range(chunks)) + (
            (fire_x, fx),
            (hrr_index, hi),
            (hrr_table, ht),
            (profile, profbuf),
            (fields.at[pl.ds(1, spec), pl.ds(XL - 2, 2)], tail),
            (fields.at[pl.ds(2, 3)], fbuf.at[pl.ds(2, 3)]),
        ))
    ]
    for copy in loads:
        copy.start()
    velocity_loads, down_loads, small_loads, load_rest = loads[:4], loads[4:-6], loads[-6:-1], loads[-1]

    lane = lax.broadcasted_iota(jnp.int32, (rows, 128), 1)
    not_first = lane > 0
    not_last = lane < 127

    def along_height(f):
        return jnp.where(not_first, pltpu.roll(f, 1, 1), 0.0) + jnp.where(not_last, pltpu.roll(f, 127, 1), 0.0)

    half = 0.5 * time_step
    keep = 1.0 - 2.0 * kappa_along - 2.0 * diffusivity_depth
    for copy in velocity_loads:
        copy.wait()
    for q in range(NXD):
        part = slice(q * quarter, (q + 1) * quarter)
        se[q, 0:quarter] = fbuf[0, 0, part]
        se[q, quarter : 2 * quarter] = fbuf[0, XL - 1, part]

    def velocity(k, ahead, behind):
        u = fbuf[0, k]
        bend = half * u
        star = (time_step * buoyancy) * fbuf[1, k] + diffusivity_depth * (u + along_height(u))
        if ahead is not None:
            star = star + ahead * (kappa_along - bend)
        if behind is not None:
            star = star + behind * (kappa_along + bend)
        return star

    def two_sided():
        star = velocity(0, fbuf[0, 1], None)
        ubuf[0] = star
        near_out[0, 0] = star

        def forward(n, f):
            for k in (2 * n + 1, 2 * n + 2):
                star = velocity(k, fbuf[0, k + 1], fbuf[0, k - 1])
                f = ROOT * f + star
                ubuf[k] = star
                near_out[0, k] = f
            return f

        f = lax.fori_loop(0, (XL - 2) // 2, forward, star)
        star = velocity(XL - 1, None, fbuf[0, XL - 2])
        ubuf[XL - 1] = star
        near_out[0, XL - 1] = ROOT * f + star

        def backward(n, b):
            for k in (XL - 1 - 2 * n, XL - 2 - 2 * n):
                near_out[0, k] = GAIN * (near_out[0, k] + ROOT * b)
                b = ubuf[k] + ROOT * b
            return b

        lax.fori_loop(0, XL // 2, backward, jnp.zeros((rows, 128), jnp.float32))

    early = z < NZD // 2

    @pl.when(early)
    def _():
        two_sided()

    extra = 4 * jnp.where((x == 0) & (z > 0), 1, 0) + 4 * jnp.where((x == last_x) & (z < last_z), 1, 0)
    pl.semaphore_wait(barrier, NXD - 1 + NZD - 1 + extra)

    sends = []

    def to_row(out, into, send, recv):
        for k in (2, 1, 3):
            to = lax.rem(x + k, NXD)
            copy = remote(out.at[to], into.at[x], send.at[k - 1], recv.at[x], z * NXD + to)
            copy.start()
            sends.append(copy)

    def from_row(into, send, recv):
        for k in range(1, NXD):
            source = lax.rem(x + k, NXD)
            remote(into.at[source], into.at[source], send.at[0], recv.at[source], me).wait_recv()

    def to_column(out, into, send, recv):
        for k in (4, 3, 5, 2, 6, 1, 7):
            to = lax.rem(z + k, NZD)
            copy = remote(out.at[jnp.where(to > z, 0, 1)], into.at[z], send.at[k - 1], recv.at[z], to * NXD + x)
            copy.start()
            sends.append(copy)

    def from_column(into, send, recv):
        for k in range(1, NZD):
            source = lax.rem(z + k, NZD)
            remote(into.at[source], into.at[source], send.at[0], recv.at[source], me).wait_recv()

    def crossing(low):
        target = (z - 1 if low else z + 1) * NXD
        return [
            remote(se.at[q, pl.ds(0 if low else quarter, quarter)], cross.at[1 if low else 0],
                   ssc.at[0 if low else 1, q], rsc.at[1 if low else 0], target + q)
            for q in range(NXD)
        ]

    @pl.when((x == 0) & (z > 0))
    def _():
        for copy in crossing(True):
            copy.start()

    @pl.when((x == last_x) & (z < last_z))
    def _():
        for copy in crossing(False):
            copy.start()

    to_row(se, re, sse, rse)

    block = rows // 2
    for part in range(2):
        at = slice(part * block, (part + 1) * block)
        first = fbuf[0, 0, at]
        behind, here = None, first
        for k in range(XL):
            ahead = fbuf[0, k + 1, at] if k < XL - 1 else None
            if behind is None:
                bent = fbuf[1, k, at] - here * ahead
                up_u, up_b, down_u, down_b = here, bent, here, bent
            else:
                slope = behind if ahead is None else behind - ahead
                bent = fbuf[1, k, at] + here * slope
                up_u, up_b = ROOT * up_u + here, ROOT * up_b + bent
                down_u, down_b = down_u + power(k) * here, down_b + power(k) * bent
            behind, here = here, ahead
        final = behind
        ends = (
            (up_u, up_b, ROOT * (up_u - power(XL - 1) * first) + (1.0 / ROOT) * (up_u - final)),
            (down_u, down_b, (1.0 / ROOT) * (down_u - first) + ROOT * (down_u - power(XL - 1) * final)),
        )
        for side, (plain, bent, shifted) in enumerate(ends):
            inside = lax.broadcasted_iota(jnp.int32, (block, 128), 1)
            high = jnp.where(inside > 0, pltpu.roll(plain, 1, 1), 0.0) + jnp.where(inside < 127, pltpu.roll(plain, 127, 1), 0.0)
            total = half * bent + keep * plain + kappa_along * shifted + diffusivity_depth * high
            for i in range(block // quarter):
                s1[part * (block // quarter) + i, side * quarter : (side + 1) * quarter] = total[i * quarter : (i + 1) * quarter]

    to_row(s1, r1, ss1, rs1)

    for copy in down_loads:
        copy.wait()
    segments = dbuf.shape[2] // SEG
    for s in range(segments):
        for p in range(spec):
            wseg[p, s : s + 1] = wallbuf[p, pl.ds(sg[s], 1)]
    sub = lax.broadcasted_iota(jnp.int32, (segments, 128), 0)
    for r, (p, c) in enumerate(lines):
        cols = slice(c * 128, (c + 1) * 128)
        col = courbuf[p : p + 1, cols]
        factor = 1.0 / ((1.0 + col) * (1.0 + wseg[p, :, cols]))
        fac[r] = factor
        rate[r] = col * factor
    state = [jnp.zeros((segments, 128), jnp.float32) for _ in lines]
    for j in range(SEG):
        for r, (p, c) in enumerate(lines):
            state[r] = rate[r] * state[r] + fac[r] * dbuf[p, c, pl.ds(j, segments, stride=SEG), :]
    passed = [rate[r] for r in range(len(lines))]
    for _ in range(4):
        passed = [a * a for a in passed]
    for shift in (1, 2, 4):
        ok = sub >= shift
        for r in range(len(lines)):
            a_prev = jnp.where(ok, pltpu.roll(passed[r], shift, 0), 1.0)
            h_prev = jnp.where(ok, pltpu.roll(state[r], shift, 0), 0.0)
            state[r] = passed[r] * h_prev + state[r]
            passed[r] = passed[r] * a_prev
    zero_rows = jnp.zeros((d1.shape[1], 128), jnp.float32)
    for q in range(NXD):
        d1[q] = zero_rows
        d3[q] = zero_rows
    for r in range(len(lines)):
        pre_a[r] = jnp.where(sub >= 1, pltpu.roll(passed[r], 1, 0), 1.0)
        pre_h[r] = jnp.where(sub >= 1, pltpu.roll(state[r], 1, 0), 0.0)
        q, i = divmod(r, per)
        d1[q, i : i + 1] = passed[r][segments - 1 : segments]
        d1[q, per + i : per + i + 1] = state[r][segments - 1 : segments]

    for copy in small_loads:
        copy.wait()
    fires = [(fx[i] - me * XL, ht[hi[i]] * time_step) for i in range(fx.shape[0])]

    def heat_at(k):
        total = jnp.float32(0.0)
        for place, release in fires:
            total = total + jnp.where(place == k, release, 0.0)
        return total

    def transported(f, u, ahead, behind, heat):
        bend = half * u
        return ahead * (kappa_along - bend) + behind * (kappa_along + bend) + diffusivity_depth * (f + along_height(f)) + heat

    @pl.when(me == last)
    def _():
        heat = heat_at(XL - 1) * profbuf[...]
        from_lane = lax.broadcasted_iota(jnp.int32, (128, 128), 0)
        to_lane = lax.broadcasted_iota(jnp.int32, (128, 128), 1)
        pool = jnp.where(from_lane // 4 == lax.rem(to_lane, 32), 1.0 / 16.0, 0.0)
        row = lax.broadcasted_iota(jnp.int32, (rows, 128), 0)
        kept = lax.rem(row, 16) // 4 == lane // 32
        for p in range(spec):
            layer = transported(tail[p, 1], fbuf[0, XL - 1], jnp.zeros((rows, 128), jnp.float32), tail[p, 0], source_yields[p + 1] * heat)
            pooled = jnp.dot(layer, pool, precision=lax.Precision.HIGHEST, preferred_element_type=jnp.float32)
            pooled = jnp.where(kept, pooled, 0.0)
            for c in range(chunks):
                q, i = divmod(p * chunks + c, per)
                d1[q, per + i : per + i + 1] = jnp.sum(pooled[16 * c : 16 * c + 16], axis=0, keepdims=True)

    to_row(d1, e1, sd1, rd1)
    re[x] = se[x]
    r1[x] = s1[x]
    e1[x] = d1[x]

    load_rest.wait()

    def inner(members):
        def layer(k):
            heat = heat_at(k)
            u = fbuf[0, k]
            bend = half * u
            before, after = kappa_along + bend, kappa_along - bend
            shape = profbuf[...]
            for i in members:
                f = fbuf[i, k]
                moved = fbuf[i, k + 1] * after + fbuf[i, k - 1] * before + diffusivity_depth * (f + along_height(f))
                near_out[i, k] = moved + (source_yields[i] * heat) * shape

        def pair(n, carry):
            layer(2 * n + 1)
            layer(2 * n + 2)
            return carry

        lax.fori_loop(0, (XL - 2) // 2, pair, 0)

    inner((1, 2))

    from_row(re, sse, rse)

    @pl.when(z > 0)
    def _():
        remote(cross.at[0], cross.at[0], ssc.at[0, 0], rsc.at[0], me).wait_recv()

    @pl.when(z == 0)
    def _():
        cross[0] = jnp.zeros((quarter, 128), jnp.float32)

    @pl.when(z < last_z)
    def _():
        remote(cross.at[1], cross.at[1], ssc.at[0, 0], rsc.at[1], me).wait_recv()

    @pl.when(z == last_z)
    def _():
        cross[1] = jnp.zeros((quarter, 128), jnp.float32)

    from_row(r1, ss1, rs1)
    lows = [re[i, 0:quarter] for i in range(NXD)]
    highs = [re[i, quarter : 2 * quarter] for i in range(NXD)]
    sum_f, sum_b = [], []
    for i in range(NXD):
        before = cross[0] if i == 0 else highs[i - 1]
        after = cross[1] if i == NXD - 1 else lows[i + 1]
        at_low = before * (kappa_along + half * lows[i])
        at_high = after * (kappa_along - half * highs[i])
        sum_f.append(r1[i, 0:quarter] + power(XL - 1) * at_low + at_high)
        sum_b.append(r1[i, quarter : 2 * quarter] + at_low + power(XL - 1) * at_high)
    group_f = sum_f[0]
    for i in range(1, NXD):
        group_f = power(XL) * group_f + sum_f[i]
    group_b = sum_b[NXD - 1]
    for i in reversed(range(NXD - 1)):
        group_b = power(XL) * group_b + sum_b[i]
    s2[0] = ROUND * (group_f + pick([power(GROUP + 2 + 2 * GROUP * i) for i in range(NZD)], z) * group_b)
    s2[1] = ROUND * (group_b + pick([power(GROUP * (2 * NZD - 1) - 2 * GROUP * i) for i in range(NZD)], z) * group_f)
    to_column(s2, r2, ss2, rs2)

    from_row(e1, sd1, rd1)
    rates = [e1[i, 0:per] for i in range(NXD)]
    drives = [e1[i, per : 2 * per] for i in range(NXD)]
    group_a, group_h = rates[0], drives[0]
    for i in range(1, NXD):
        group_a, group_h = rates[i] * group_a, rates[i] * group_h + drives[i]
    for side in range(2):
        d2[side] = zero_rows
        d2[side, 0:per] = group_a
        d2[side, per : 2 * per] = jnp.where(z == last_z, drives[NXD - 1], group_h)
    to_column(d2, e2, sd2, rd2)
    r2[z] = s2[0]
    e2[z] = d2[0]

    up = remote(fbuf.at[:, pl.ds(XL - 1, 1)], halo.at[0], ssh.at[0], rsh.at[0], me + 1)
    low = remote(fbuf.at[:, pl.ds(0, 1)], halo.at[1], ssh.at[1], rsh.at[1], me - 1)

    @pl.when(me < last)
    def _():
        up.start()

    @pl.when(me > 0)
    def _():
        low.start()

    inner((3, 4))

    @pl.when(jnp.logical_not(early))
    def _():
        two_sided()

    from_column(r2, ss2, rs2)
    in_f = ROUND * (pick([power(2 * GROUP * i + 2) for i in range(NZD)], z) * group_b + power(2 * LENGTH - GROUP + 2) * group_f)
    in_b = ROUND * (pick([power(2 * GROUP * (NZD - 1 - i)) for i in range(NZD)], z) * group_f + power(2 * LENGTH - GROUP + 2) * group_b)
    for s in range(NZD):
        part = r2[s]
        coef_f = pick([from_below_f(i, s) if s < i else from_above_f(i, s) if s > i else 0.0 for i in range(NZD)], z)
        coef_b = pick([from_below_b(i, s) if s < i else from_above_b(i, s) if s > i else 0.0 for i in range(NZD)], z)
        in_f = in_f + coef_f * part
        in_b = in_b + coef_b * part
    f_at, b_at = in_f, in_b
    for i in range(NXD):
        s3[i, 0:quarter] = f_at
        f_at = power(XL) * f_at + sum_f[i]
    for i in reversed(range(NXD)):
        s3[i, quarter : 2 * quarter] = b_at
        b_at = power(XL) * b_at + sum_b[i]
    to_row(s3, r3, ss3, rs3)

    from_column(e2, sd2, rd2)
    arrive = e2[last_z, per : 2 * per]
    for s in range(NZD - 1):
        passed_on = e2[s, 0:per] * arrive + e2[s, per : 2 * per]
        arrive = jnp.where(s < z, passed_on, arrive)
    for i in range(NXD):
        d3[i, 0:per] = arrive
        arrive = rates[i] * arrive + drives[i]
    to_row(d3, e3, sd3, rd3)
    r3[x] = s3[x]
    e3[x] = d3[x]

    @pl.when(me > 0)
    def _():
        remote(halo.at[0], halo.at[0], ssh.at[0], rsh.at[0], me).wait_recv()

    @pl.when(me == 0)
    def _():
        halo[0] = jnp.zeros(halo.shape[1:], jnp.float32)

    @pl.when(me < last)
    def _():
        remote(halo.at[1], halo.at[1], ssh.at[0], rsh.at[1], me).wait_recv()

    @pl.when(me == last)
    def _():
        halo[1] = jnp.zeros(halo.shape[1:], jnp.float32)

    heat_low = heat_at(0) * profbuf[...]
    heat_high = heat_at(XL - 1) * profbuf[...]
    for i in range(1, 5):
        near_out[i, 0] = transported(fbuf[i, 0], fbuf[0, 0], fbuf[i, 1], halo[0, i, 0], source_yields[i] * heat_low)
        near_out[i, XL - 1] = transported(fbuf[i, XL - 1], fbuf[0, XL - 1], halo[1, i, 0], fbuf[i, XL - 2], source_yields[i] * heat_high)

    from_row(r3, ss3, rs3)
    from_low = jnp.concatenate([r3[q, 0:quarter] for q in range(NXD)], axis=0)
    from_high = jnp.concatenate([r3[q, quarter : 2 * quarter] for q in range(NXD)], axis=0)
    edges[0] = GAIN * (ROOT * from_low + halo[0, 0, 0] * (kappa_along + half * fbuf[0, 0]))
    edges[1] = GAIN * (ROOT * from_high + halo[1, 0, 0] * (kappa_along - half * fbuf[0, XL - 1]))
    from_row(e3, sd3, rd3)
    for r in range(len(lines)):
        q, i = divmod(r, per)
        start[r] = pre_a[r] * e3[q, i : i + 1] + pre_h[r]

    for copy in sends:
        copy.wait_send()

    @pl.when((x == 0) & (z > 0))
    def _():
        for copy in crossing(True):
            copy.wait_send()

    @pl.when((x == last_x) & (z < last_z))
    def _():
        for copy in crossing(False):
            copy.wait_send()

    @pl.when(me < last)
    def _():
        up.wait_send()

    @pl.when(me > 0)
    def _():
        low.wait_send()


def write_kernel(near_in, edges, dbuf, fac, rate, start, near_out, down_out, velocity, dnext, sem):
    copies = [
        pltpu.make_async_copy(near_in.at[i, pl.ds(h * 16, 16)], near_out.at[i, pl.ds(h * 16, 16)], sem.at[2 * i + h])
        for i in range(1, 5) for h in range(2)
    ]
    for copy in copies:
        copy.start()
    spec, chunks = dbuf.shape[:2]
    segments = dbuf.shape[2] // SEG
    for c in range(chunks):
        state = [start[p * chunks + c] for p in range(spec)]
        for j in range(SEG):
            at = pl.ds(j, segments, stride=SEG)
            for p in range(spec):
                r = p * chunks + c
                state[p] = rate[r] * state[p] + fac[r] * dbuf[p, c, at, :]
                dnext[p, c, at, :] = state[p]
        copy = pltpu.make_async_copy(dnext.at[:, c], down_out.at[:, :, pl.ds(128 * c, 128)], sem.at[10 + c])
        copy.start()
        copies.append(copy)
    for part in range(2):
        for k in range(16 * part, 16 * part + 16):
            velocity[k] = near_in[0, k] + (power(k) * edges[0] + power(XL - 1 - k) * edges[1])
        copy = pltpu.make_async_copy(velocity.at[pl.ds(16 * part, 16)], near_out.at[0, pl.ds(16 * part, 16)], sem.at[part])
        copy.start()
        copies.append(copy)
    for copy in copies:
        copy.wait()


def body(fields, down_state, fire_x, hrr_index, hrr_table, profile, courant, wall_loss, seg_table):
    f32 = jnp.float32
    rows = fields.shape[2]
    quarter = rows // NXD
    spec, cells, columns = down_state.shape
    segments = cells // SEG
    lines = spec * columns // 128
    per = lines // NXD

    small = -(-2 * per // 8) * 8
    vmem, smem, dma = pltpu.VMEM, pltpu.SMEM, pltpu.SemaphoreType.DMA
    hbm = pl.BlockSpec(memory_space=pltpu.HBM)
    in_vmem = pl.BlockSpec(memory_space=pltpu.VMEM)
    chunked = (spec, columns // 128, cells, 128)
    shapes = (fields.shape, (2, rows, 128), chunked) + ((lines, segments, 128),) * 3
    middle = pl.pallas_call(
        tunnel_kernel,
        out_shape=tuple(jax.ShapeDtypeStruct(shape, f32) for shape in shapes),
        in_specs=[hbm] * 9,
        out_specs=(in_vmem,) * len(shapes),
        scratch_shapes=[
            vmem(fields.shape, f32),
            vmem(fields.shape[1:], f32),
            vmem((2, 5, 1, rows, 128), f32),
            vmem((spec, 2, rows, 128), f32),
            vmem((spec, wall_loss.shape[0], columns), f32),
            vmem(courant.shape, f32),
            vmem(profile.shape, f32),
            vmem((NXD, 2 * quarter, 128), f32),
            vmem((NXD, 2 * quarter, 128), f32),
            vmem((NXD, 2 * quarter, 128), f32),
            vmem((NXD, 2 * quarter, 128), f32),
            vmem((2, quarter, 128), f32),
            vmem((2, quarter, 128), f32),
            vmem((NZD, quarter, 128), f32),
            vmem((NXD, 2 * quarter, 128), f32),
            vmem((NXD, 2 * quarter, 128), f32),
            vmem((NXD, small, 128), f32),
            vmem((NXD, small, 128), f32),
            vmem((2, small, 128), f32),
            vmem((NZD, small, 128), f32),
            vmem((NXD, small, 128), f32),
            vmem((NXD, small, 128), f32),
            vmem((spec, segments, columns), f32),
            vmem((lines, segments, 128), f32),
            vmem((lines, segments, 128), f32),
            smem(fire_x.shape, jnp.int32),
            smem(hrr_index.shape, jnp.int32),
            smem(hrr_table.shape, f32),
            smem(seg_table.shape, jnp.int32),
            dma((17,)),
            dma((NXD - 1,)),
            dma((NXD,)),
            dma((NXD - 1,)),
            dma((NXD,)),
            dma((2, NXD)),
            dma((2,)),
            dma((2,)),
            dma((2,)),
            dma((NZD - 1,)),
            dma((NZD,)),
            dma((NXD - 1,)),
            dma((NXD,)),
            dma((NXD - 1,)),
            dma((NXD,)),
            dma((NZD - 1,)),
            dma((NZD,)),
            dma((NXD - 1,)),
            dma((NXD,)),
        ],
        compiler_params=pltpu.CompilerParams(
            collective_id=0, has_side_effects=True, vmem_limit_bytes=32 * 1024 * 1024
        ),
        name="tunnel_step",
    )(*(pltpu.with_memory_space_constraint(a, pltpu.HBM) for a in (fields, down_state, fire_x, hrr_index, hrr_table, profile, courant, jnp.transpose(wall_loss, (1, 0, 2)), seg_table)))
    return pl.pallas_call(
        write_kernel,
        out_shape=(jax.ShapeDtypeStruct(fields.shape, f32), jax.ShapeDtypeStruct(down_state.shape, f32)),
        in_specs=[in_vmem] * len(shapes),
        out_specs=(hbm, hbm),
        scratch_shapes=[vmem(fields.shape[1:], f32), vmem(chunked, f32), dma((14,))],
        compiler_params=pltpu.CompilerParams(vmem_limit_bytes=16 * 1024 * 1024),
        name="write_out",
    )(*middle)


def solution(mesh):
    placed = (
        P("scen", "near", "sect", None),
        P("scen", "near", "sect"),
        P("scen"),
        P("scen"),
        P(),
        P("sect", None),
        P(None, "sect"),
        P(None, None, "sect"),
        P("near"),
    )
    return jax.shard_map(
        body,
        mesh=mesh,
        in_specs=placed,
        out_specs=(P("scen", "near", "sect", None), P("scen", "near", "sect")),
        check_vma=False,
    )
```

time: 30.6 us -> 25.4 us (0.83)
  Pallas kernels: 29.8 us -> 24.7 us
    pallas_call x1, Pallas kernels: 27.1 us -> 22 us  [body(): pl.pallas_call(tunnel_kernel, out_shape=tuple((jax.ShapeDtypeStruct(shape...]
where the time goes in v1:
time: 25.4 us
  Pallas kernels  24.7 us (97%)
  between operations  0.64 us (3%)
    pallas_call x1, Pallas kernels, body(): pl.pallas_call(tunnel_kernel, out_shape=tuple((jax.ShapeDtypeStruct(shape...  22 us
    pallas_call x1, Pallas kernels, body(): pl.pallas_call(write_kernel, out_shape=(jax.ShapeDtypeStruct(fields.shape...  2.69 us

profile of v1, /device:TPU:8, one launch (start us, length us, event | category | flops | bytes accessed | tf_op | source)
XLA Modules:
  0.0 25.4 jit_solution(3020111995392929099)
XLA Ops:
  0.6 22.0 %tunnel_step.1 = (f32[5,32,64,128]{3,2,1,0:T(8,128)S(1)}, f32[2,64,128]{2,1,0:T(8,128)S(1)}, f32[3,4,128,128]{3,2,1,0:T(8,128)S(1)}, f32[12,8,128]{2,1,0:T(8,128...) custom-call(f32[5,32,64,128]{3,2,1,0:T(8,128)} %fields.1, f32[3,128,512]{2,1,0:T(8,128)} %down.1, s32[4]{0:T(128)} %fire_x.1, ...), custom_call_target="tpu_custom_call" | custom-call | tf_op jit(solution)/shard_map/tunnel_step/pallas_call | solution.py:559
  22.7 2.7 %write_out.1 = (f32[5,32,64,128]{3,2,1,0:T(8,128)}, f32[3,128,512]{2,1,0:T(8,128)}) custom-call(f32[5,32,64,128]{3,2,1,0:T(8,128)S(1)} %get-tuple-element.8.near_in, f32[2,64,128]{2,1,0:T(8,128)S(1)} %get-tuple-element.9.edges, f32[3,4,128,128]{3,2,1,0:T(8,128)S(1)} %get-tuple-element.10.dbuf, f32[12,8,128]{2,1,0:T(8,128)S(1)} %get-tuple-element.11.fac, ...), custom_call_target="tpu_custom_call" | custom-call | tf_op jit(solution)/shard_map/write_out/pallas_call | solution.py:619

commit v2 on v1

--- a/solution.py
+++ b/solution.py
@@ -34,6 +34,8 @@
 ROUND = 1.0 / (1.0 - power(2 * LENGTH + 2))
 GROUP = XL * NXD
 
+FAR = (3, 4, 5)
+
 
 def pick(values, index):
     chosen = jnp.float32(values[0])
@@ -62,10 +64,13 @@
     fields, down, fire_x, hrr_index, hrr_table, profile, courant, wall, seg,
     near_out, edges, dbuf, fac, rate, start,
     fbuf, ubuf, halo, tail, wallbuf, courbuf, profbuf,
-    se, re, s1, r1, cross, s2, r2, s3, r3, d1, e1, d2, e2, d3, e3, wseg, pre_a, pre_h,
+    s1, r1, cross, s2, r2, s3, r3, r4, total, carry, d1, e1, d2, e2, d3, e3, wseg, pre_a, pre_h,
     fx, hi, ht, sg,
-    load_sem, sse, rse, ss1, rs1, ssc, rsc, ssh, rsh, ss2, rs2, ss3, rs3, sd1, rd1, sd2, rd2, sd3, rd3,
+    load_sem, ss1, rs1, ssc, rsc, ssh, rsh, ss2, rs2, ss3, rs3, ss4, rs4, sd1, rd1, sd2, rd2, sd3, rd3,
 ):
+    velocity_loads = [pltpu.make_async_copy(fields.at[f], fbuf.at[f], load_sem.at[f]) for f in range(2)]
+    for copy in velocity_loads:
+        copy.start()
     me = lax.axis_index("near")
     z = me // NXD
     x = lax.rem(me, NXD)
@@ -88,11 +93,19 @@
     def greet(target):
         pl.semaphore_signal(barrier, inc=1, device_id={"near": target}, device_id_type=MESH)
 
-    for k in range(1, NZD):
+    for k in (4, 3, 5, 2, 6, 1, 7):
         greet(lax.rem(z + k, NZD) * NXD + x)
-    for k in range(1, NXD):
+    for k in (2, 1, 3):
         greet(z * NXD + lax.rem(x + k, NXD))
 
+    @pl.when(z == 0)
+    def _():
+        for k in (1, 2, 3):
+            for far in FAR:
+                greet(far * NXD + lax.rem(x + k, NXD))
+
+    is_far = (z >= FAR[0]) & (z <= FAR[-1])
+
     @pl.when(z < last_z)
     def _():
         greet((z + 1) * NXD)
@@ -101,13 +114,9 @@
     def _():
         greet((z - 1) * NXD + last_x)
 
-    half_layers = XL // 2
     loads = [
-        pltpu.make_async_copy(src, dst, load_sem.at[i])
-        for i, (src, dst) in enumerate(tuple(
-            (fields.at[pl.ds(f, 1), pl.ds(h * half_layers, half_layers)], fbuf.at[pl.ds(f, 1), pl.ds(h * half_layers, half_layers)])
-            for h in range(2) for f in range(2)
-        ) + (
+        pltpu.make_async_copy(src, dst, load_sem.at[2 + i])
+        for i, (src, dst) in enumerate((
             (seg, sg),
             (courant, courbuf),
             (wall, wallbuf),
@@ -122,7 +131,7 @@
     ]
     for copy in loads:
         copy.start()
-    velocity_loads, down_loads, small_loads, load_rest = loads[:4], loads[4:-6], loads[-6:-1], loads[-1]
+    down_loads, small_loads, load_rest = loads[:-6], loads[-6:-1], loads[-1]
 
     lane = lax.broadcasted_iota(jnp.int32, (rows, 128), 1)
     not_first = lane > 0
@@ -133,13 +142,6 @@
 
     half = 0.5 * time_step
     keep = 1.0 - 2.0 * kappa_along - 2.0 * diffusivity_depth
-    for copy in velocity_loads:
-        copy.wait()
-    for q in range(NXD):
-        part = slice(q * quarter, (q + 1) * quarter)
-        se[q, 0:quarter] = fbuf[0, 0, part]
-        se[q, quarter : 2 * quarter] = fbuf[0, XL - 1, part]
-
     def velocity(k, ahead, behind):
         u = fbuf[0, k]
         bend = half * u
@@ -177,13 +179,12 @@
         lax.fori_loop(0, XL // 2, backward, jnp.zeros((rows, 128), jnp.float32))
 
     early = z < NZD // 2
+    for copy in velocity_loads:
+        copy.wait()
 
     @pl.when(early)
     def _():
         two_sided()
-
-    extra = 4 * jnp.where((x == 0) & (z > 0), 1, 0) + 4 * jnp.where((x == last_x) & (z < last_z), 1, 0)
-    pl.semaphore_wait(barrier, NXD - 1 + NZD - 1 + extra)
 
     sends = []
 
@@ -214,10 +215,50 @@
     def crossing(low):
         target = (z - 1 if low else z + 1) * NXD
         return [
-            remote(se.at[q, pl.ds(0 if low else quarter, quarter)], cross.at[1 if low else 0],
-                   ssc.at[0 if low else 1, q], rsc.at[1 if low else 0], target + q)
-            for q in range(NXD)
+            remote(s1.at[k, pl.ds((2 if low else 3) * quarter, quarter)], cross.at[1 if low else 0],
+                   ssc.at[0 if low else 1, k], rsc.at[1 if low else 0], target + lax.rem(x + k, NXD))
+            for k in range(NXD)
         ]
+
+    def columns(turn):
+        return pl.ds(pl.multiple_of(lax.rem(x + turn, NXD) * quarter, quarter), quarter)
+
+    for turn in range(NXD):
+        s1[turn, 2 * quarter : 3 * quarter] = fbuf[0, 0, columns(turn)]
+        s1[turn, 3 * quarter : 4 * quarter] = fbuf[0, XL - 1, columns(turn)]
+
+    inside = lax.broadcasted_iota(jnp.int32, (quarter, 128), 1)
+
+    def local_sums(turns):
+        here = {t: fbuf[0, 0, columns(t)] for t in turns}
+        behind, total = {}, {}
+        for k in range(XL):
+            for t in turns:
+                ahead = fbuf[0, k + 1, columns(t)] if k < XL - 1 else None
+                bent = fbuf[1, k, columns(t)]
+                if k == 0:
+                    bent = bent - here[t] * ahead
+                    total[t] = (here[t], bent, here[t], bent)
+                else:
+                    bent = bent + here[t] * (behind[t] if ahead is None else behind[t] - ahead)
+                    up_u, up_b, down_u, down_b = total[t]
+                    total[t] = (ROOT * up_u + here[t], ROOT * up_b + bent, down_u + power(k) * here[t], down_b + power(k) * bent)
+                behind[t], here[t] = here[t], ahead
+        for t in turns:
+            up_u, up_b, down_u, down_b = total[t]
+            first, final = fbuf[0, 0, columns(t)], behind[t]
+            ends = (
+                (up_u, up_b, ROOT * (up_u - power(XL - 1) * first) + (1.0 / ROOT) * (up_u - final)),
+                (down_u, down_b, (1.0 / ROOT) * (down_u - first) + ROOT * (down_u - power(XL - 1) * final)),
+            )
+            for side, (plain, bent, shifted) in enumerate(ends):
+                high = jnp.where(inside > 0, pltpu.roll(plain, 1, 1), 0.0) + jnp.where(inside < 127, pltpu.roll(plain, 127, 1), 0.0)
+                s1[t, side * quarter : (side + 1) * quarter] = half * bent + keep * plain + kappa_along * shifted + diffusivity_depth * high
+
+    local_sums((2, 1, 3))
+    extra = 4 * jnp.where((x == 0) & (z > 0), 1, 0) + 4 * jnp.where((x == last_x) & (z < last_z), 1, 0)
+    extra = extra + (NXD - 1) * jnp.where(is_far, 1, 0)
+    pl.semaphore_wait(barrier, NXD - 1 + NZD - 1 + extra)
 
     @pl.when((x == 0) & (z > 0))
     def _():
@@ -229,37 +270,12 @@
         for copy in crossing(False):
             copy.start()
 
-    to_row(se, re, sse, rse)
-
-    block = rows // 2
-    for part in range(2):
-        at = slice(part * block, (part + 1) * block)
-        first = fbuf[0, 0, at]
-        behind, here = None, first
-        for k in range(XL):
-            ahead = fbuf[0, k + 1, at] if k < XL - 1 else None
-            if behind is None:
-                bent = fbuf[1, k, at] - here * ahead
-                up_u, up_b, down_u, down_b = here, bent, here, bent
-            else:
-                slope = behind if ahead is None else behind - ahead
-                bent = fbuf[1, k, at] + here * slope
-                up_u, up_b = ROOT * up_u + here, ROOT * up_b + bent
-                down_u, down_b = down_u + power(k) * here, down_b + power(k) * bent
-            behind, here = here, ahead
-        final = behind
-        ends = (
-            (up_u, up_b, ROOT * (up_u - power(XL - 1) * first) + (1.0 / ROOT) * (up_u - final)),
-            (down_u, down_b, (1.0 / ROOT) * (down_u - first) + ROOT * (down_u - power(XL - 1) * final)),
-        )
-        for side, (plain, bent, shifted) in enumerate(ends):
-            inside = lax.broadcasted_iota(jnp.int32, (block, 128), 1)
-            high = jnp.where(inside > 0, pltpu.roll(plain, 1, 1), 0.0) + jnp.where(inside < 127, pltpu.roll(plain, 127, 1), 0.0)
-            total = half * bent + keep * plain + kappa_along * shifted + diffusivity_depth * high
-            for i in range(block // quarter):
-                s1[part * (block // quarter) + i, side * quarter : (side + 1) * quarter] = total[i * quarter : (i + 1) * quarter]
-
-    to_row(s1, r1, ss1, rs1)
+    for turn in (2, 1, 3):
+        copy = remote(s1.at[turn], r1.at[x], ss1.at[turn - 1], rs1.at[x], z * NXD + lax.rem(x + turn, NXD))
+        copy.start()
+        sends.append(copy)
+    local_sums((0,))
+    r1[x] = s1[0]
 
     for copy in down_loads:
         copy.wait()
@@ -330,8 +346,6 @@
                 d1[q, per + i : per + i + 1] = jnp.sum(pooled[16 * c : 16 * c + 16], axis=0, keepdims=True)
 
     to_row(d1, e1, sd1, rd1)
-    re[x] = se[x]
-    r1[x] = s1[x]
     e1[x] = d1[x]
 
     load_rest.wait()
@@ -357,8 +371,6 @@
 
     inner((1, 2))
 
-    from_row(re, sse, rse)
-
     @pl.when(z > 0)
     def _():
         remote(cross.at[0], cross.at[0], ssc.at[0, 0], rsc.at[0], me).wait_recv()
@@ -376,8 +388,8 @@
         cross[1] = jnp.zeros((quarter, 128), jnp.float32)
 
     from_row(r1, ss1, rs1)
-    lows = [re[i, 0:quarter] for i in range(NXD)]
-    highs = [re[i, quarter : 2 * quarter] for i in range(NXD)]
+    lows = [r1[i, 2 * quarter : 3 * quarter] for i in range(NXD)]
+    highs = [r1[i, 3 * quarter : 4 * quarter] for i in range(NXD)]
     sum_f, sum_b = [], []
     for i in range(NXD):
         before = cross[0] if i == 0 else highs[i - 1]
@@ -394,6 +406,17 @@
         group_b = power(XL) * group_b + sum_b[i]
     s2[0] = ROUND * (group_f + pick([power(GROUP + 2 + 2 * GROUP * i) for i in range(NZD)], z) * group_b)
     s2[1] = ROUND * (group_b + pick([power(GROUP * (2 * NZD - 1) - 2 * GROUP * i) for i in range(NZD)], z) * group_f)
+    def to_first():
+        return [
+            remote(s2.at[1], r4.at[z - FAR[0], x], ss4.at[k - 1], rs4.at[z - FAR[0], x], lax.rem(x + k, NXD))
+            for k in (2, 1, 3)
+        ]
+
+    @pl.when(is_far)
+    def _():
+        for copy in to_first():
+            copy.start()
+
     to_column(s2, r2, ss2, rs2)
 
     from_row(e1, sd1, rd1)
@@ -427,15 +450,32 @@
     def _():
         two_sided()
 
-    from_column(r2, ss2, rs2)
-    in_f = ROUND * (pick([power(2 * GROUP * i + 2) for i in range(NZD)], z) * group_b + power(2 * LENGTH - GROUP + 2) * group_f)
-    in_b = ROUND * (pick([power(2 * GROUP * (NZD - 1 - i)) for i in range(NZD)], z) * group_f + power(2 * LENGTH - GROUP + 2) * group_b)
-    for s in range(NZD):
-        part = r2[s]
-        coef_f = pick([from_below_f(i, s) if s < i else from_above_f(i, s) if s > i else 0.0 for i in range(NZD)], z)
-        coef_b = pick([from_below_b(i, s) if s < i else from_above_b(i, s) if s > i else 0.0 for i in range(NZD)], z)
-        in_f = in_f + coef_f * part
-        in_b = in_b + coef_b * part
+    def arrived(k):
+        source = lax.rem(z + k, NZD)
+        remote(r2.at[source], r2.at[source], ss2.at[0], rs2.at[source], me).wait_recv()
+
+    def add_from(k):
+        part = r2[lax.rem(z + k, NZD)]
+        for side, (below, above) in enumerate(((from_below_f, from_above_f), (from_below_b, from_above_b))):
+            values = [below(i, (i + k) % NZD) if (i + k) % NZD < i else above(i, (i + k) % NZD) for i in range(NZD)]
+            total[side] = total[side] + pick(values, z) * part
+
+    near_rows = [k for k in range(1, NZD) if k not in FAR]
+    for k in near_rows:
+        arrived(k)
+    total[0] = ROUND * (pick([power(2 * GROUP * i + 2) for i in range(NZD)], z) * group_b + power(2 * LENGTH - GROUP + 2) * group_f)
+    total[1] = ROUND * (pick([power(2 * GROUP * (NZD - 1 - i)) for i in range(NZD)], z) * group_f + power(2 * LENGTH - GROUP + 2) * group_b)
+    for k in near_rows:
+        add_from(k)
+
+    @pl.when(z > 0)
+    def _():
+        for k in FAR:
+            arrived(k)
+        for k in FAR:
+            add_from(k)
+
+    in_f, in_b = total[0], total[1]
     f_at, b_at = in_f, in_b
     for i in range(NXD):
         s3[i, 0:quarter] = f_at
@@ -445,11 +485,30 @@
         b_at = power(XL) * b_at + sum_b[i]
     to_row(s3, r3, ss3, rs3)
 
-    from_column(e2, sd2, rd2)
-    arrive = e2[last_z, per : 2 * per]
-    for s in range(NZD - 1):
-        passed_on = e2[s, 0:per] * arrive + e2[s, per : 2 * per]
-        arrive = jnp.where(s < z, passed_on, arrive)
+    def from_row_of(k):
+        source = lax.rem(z + k, NZD)
+        remote(e2.at[source], e2.at[source], sd2.at[0], rd2.at[source], me).wait_recv()
+
+    @pl.when(z > 0)
+    def _():
+        for k in range(1, NZD):
+            from_row_of(k)
+
+    @pl.when(z == 0)
+    def _():
+        from_row_of(last_z)
+
+    carry[0:per] = e2[last_z, per : 2 * per]
+
+    @pl.when(z > 0)
+    def _():
+        arrive = carry[0:per]
+        for s in range(NZD - 1):
+            passed_on = e2[s, 0:per] * arrive + e2[s, per : 2 * per]
+            arrive = jnp.where(s < z, passed_on, arrive)
+        carry[0:per] = arrive
+
+    arrive = carry[0:per]
     for i in range(NXD):
         d3[i, 0:per] = arrive
         arrive = rates[i] * arrive + drives[i]
@@ -484,6 +543,29 @@
     from_high = jnp.concatenate([r3[q, quarter : 2 * quarter] for q in range(NXD)], axis=0)
     edges[0] = GAIN * (ROOT * from_low + halo[0, 0, 0] * (kappa_along + half * fbuf[0, 0]))
     edges[1] = GAIN * (ROOT * from_high + halo[1, 0, 0] * (kappa_along - half * fbuf[0, XL - 1]))
+
+    @pl.when(z == 0)
+    def _():
+        for k in range(1, last_z):
+            from_row_of(k)
+        for far in FAR:
+            arrived(far)
+            for k in (1, 2, 3):
+                source = lax.rem(x + k, NXD)
+                remote(r4.at[far - FAR[0], source], r4.at[far - FAR[0], source], ss4.at[0], rs4.at[far - FAR[0], source], me).wait_recv()
+            r4[far - FAR[0], x] = r2[far]
+        along = pick([power(XL * i) for i in range(NXD)], x)
+        against = pick([power(XL * (NXD - 1 - i)) for i in range(NXD)], x)
+        for q in range(NXD):
+            part = slice(q * quarter, (q + 1) * quarter)
+            up_sum = from_above_f(0, FAR[0]) * r4[0, q]
+            down_sum = from_above_b(0, FAR[0]) * r4[0, q]
+            for far in FAR[1:]:
+                up_sum = up_sum + from_above_f(0, far) * r4[far - FAR[0], q]
+                down_sum = down_sum + from_above_b(0, far) * r4[far - FAR[0], q]
+            edges[0, part] = edges[0, part] + (GAIN * ROOT) * along * up_sum
+            edges[1, part] = edges[1, part] + (GAIN * ROOT) * against * down_sum
+
     from_row(e3, sd3, rd3)
     for r in range(len(lines)):
         q, i = divmod(r, per)
@@ -491,6 +573,11 @@
 
     for copy in sends:
         copy.wait_send()
+
+    @pl.when(is_far)
+    def _():
+        for copy in to_first():
+            copy.wait_send()
 
     @pl.when((x == 0) & (z > 0))
     def _():
@@ -569,15 +656,16 @@
             vmem((spec, wall_loss.shape[0], columns), f32),
             vmem(courant.shape, f32),
             vmem(profile.shape, f32),
-            vmem((NXD, 2 * quarter, 128), f32),
-            vmem((NXD, 2 * quarter, 128), f32),
-            vmem((NXD, 2 * quarter, 128), f32),
-            vmem((NXD, 2 * quarter, 128), f32),
+            vmem((NXD, 4 * quarter, 128), f32),
+            vmem((NXD, 4 * quarter, 128), f32),
             vmem((2, quarter, 128), f32),
             vmem((2, quarter, 128), f32),
             vmem((NZD, quarter, 128), f32),
             vmem((NXD, 2 * quarter, 128), f32),
             vmem((NXD, 2 * quarter, 128), f32),
+            vmem((len(FAR), NXD, quarter, 128), f32),
+            vmem((2, quarter, 128), f32),
+            vmem((small, 128), f32),
             vmem((NXD, small, 128), f32),
             vmem((NXD, small, 128), f32),
             vmem((2, small, 128), f32),
@@ -591,9 +679,7 @@
             smem(hrr_index.shape, jnp.int32),
             smem(hrr_table.shape, f32),
             smem(seg_table.shape, jnp.int32),
-            dma((17,)),
-            dma((NXD - 1,)),
-            dma((NXD,)),
+            dma((15,)),
             dma((NXD - 1,)),
             dma((NXD,)),
             dma((2, NXD)),
@@ -604,6 +690,8 @@
             dma((NZD,)),
             dma((NXD - 1,)),
             dma((NXD,)),
+            dma((NXD - 1,)),
+            dma((len(FAR), NXD)),
             dma((NXD - 1,)),
             dma((NXD,)),
             dma((NZD - 1,)),

time: 25.4 us -> 24.4 us (0.961)
  Pallas kernels: 24.7 us -> 23.6 us
    pallas_call x1, Pallas kernels: 22 us -> 20.9 us  [body(): pl.pallas_call(tunnel_kernel, out_shape=tuple((jax.ShapeDtypeStruct(shape...]
where the time goes in v2:
time: 24.4 us; the launch traced here: 24.2 us
  Pallas kernels  23.6 us (97%)
  between operations  0.64 us (3%)
    pallas_call x1, Pallas kernels, body(): pl.pallas_call(tunnel_kernel, out_shape=tuple((jax.ShapeDtypeStruct(shape...  20.9 us
    pallas_call x1, Pallas kernels, body(): pl.pallas_call(write_kernel, out_shape=(jax.ShapeDtypeStruct(fields.shape...  2.69 us

profile of v2, /device:TPU:8, one launch (start us, length us, event | category | flops | bytes accessed | tf_op | source)
XLA Modules:
  0.0 24.2 jit_solution(14269551556819127434)
XLA Ops:
  0.6 20.9 %tunnel_step.1 = (f32[5,32,64,128]{3,2,1,0:T(8,128)S(1)}, f32[2,64,128]{2,1,0:T(8,128)S(1)}, f32[3,4,128,128]{3,2,1,0:T(8,128)S(1)}, f32[12,8,128]{2,1,0:T(8,128...) custom-call(f32[5,32,64,128]{3,2,1,0:T(8,128)} %fields.1, f32[3,128,512]{2,1,0:T(8,128)} %down.1, s32[4]{0:T(128)} %fire_x.1, ...), custom_call_target="tpu_custom_call" | custom-call | tf_op jit(solution)/shard_map/tunnel_step/pallas_call | solution.py:646
  21.5 2.7 %write_out.1 = (f32[5,32,64,128]{3,2,1,0:T(8,128)}, f32[3,128,512]{2,1,0:T(8,128)}) custom-call(f32[5,32,64,128]{3,2,1,0:T(8,128)S(1)} %get-tuple-element.8.near_in, f32[2,64,128]{2,1,0:T(8,128)S(1)} %get-tuple-element.9.edges, f32[3,4,128,128]{3,2,1,0:T(8,128)S(1)} %get-tuple-element.10.dbuf, f32[12,8,128]{2,1,0:T(8,128)S(1)} %get-tuple-element.11.fac, ...), custom_call_target="tpu_custom_call" | custom-call | tf_op jit(solution)/shard_map/write_out/pallas_call | solution.py:707

commit v3 on v2

--- a/solution.py
+++ b/solution.py
@@ -34,7 +34,8 @@
 ROUND = 1.0 / (1.0 - power(2 * LENGTH + 2))
 GROUP = XL * NXD
 
-FAR = (3, 4, 5)
+FAR = (4, 5)
+FIRST = 1
 
 
 def pick(values, index):
@@ -98,13 +99,13 @@
     for k in (2, 1, 3):
         greet(z * NXD + lax.rem(x + k, NXD))
 
-    @pl.when(z == 0)
+    @pl.when(z < FIRST)
     def _():
         for k in (1, 2, 3):
             for far in FAR:
-                greet(far * NXD + lax.rem(x + k, NXD))
-
-    is_far = (z >= FAR[0]) & (z <= FAR[-1])
+                greet((z + far) * NXD + lax.rem(x + k, NXD))
+
+    far_pairs = [(t, i) for t in range(FIRST) for i in range(len(FAR))]
 
     @pl.when(z < last_z)
     def _():
@@ -257,7 +258,8 @@
 
     local_sums((2, 1, 3))
     extra = 4 * jnp.where((x == 0) & (z > 0), 1, 0) + 4 * jnp.where((x == last_x) & (z < last_z), 1, 0)
-    extra = extra + (NXD - 1) * jnp.where(is_far, 1, 0)
+    for t, i in far_pairs:
+        extra = extra + (NXD - 1) * jnp.where(z == t + FAR[i], 1, 0)
     pl.semaphore_wait(barrier, NXD - 1 + NZD - 1 + extra)
 
     @pl.when((x == 0) & (z > 0))
@@ -406,16 +408,18 @@
         group_b = power(XL) * group_b + sum_b[i]
     s2[0] = ROUND * (group_f + pick([power(GROUP + 2 + 2 * GROUP * i) for i in range(NZD)], z) * group_b)
     s2[1] = ROUND * (group_b + pick([power(GROUP * (2 * NZD - 1) - 2 * GROUP * i) for i in range(NZD)], z) * group_f)
-    def to_first():
+    def to_first(t, i):
         return [
-            remote(s2.at[1], r4.at[z - FAR[0], x], ss4.at[k - 1], rs4.at[z - FAR[0], x], lax.rem(x + k, NXD))
+            remote(s2.at[1], r4.at[i, x], ss4.at[i, k - 1], rs4.at[i, x], t * NXD + lax.rem(x + k, NXD))
             for k in (2, 1, 3)
         ]
 
-    @pl.when(is_far)
-    def _():
-        for copy in to_first():
-            copy.start()
+    for t, i in far_pairs:
+
+        @pl.when(z == t + FAR[i])
+        def _():
+            for copy in to_first(t, i):
+                copy.start()
 
     to_column(s2, r2, ss2, rs2)
 
@@ -468,7 +472,7 @@
     for k in near_rows:
         add_from(k)
 
-    @pl.when(z > 0)
+    @pl.when(z >= FIRST)
     def _():
         for k in FAR:
             arrived(k)
@@ -485,28 +489,22 @@
         b_at = power(XL) * b_at + sum_b[i]
     to_row(s3, r3, ss3, rs3)
 
-    def from_row_of(k):
+    def from_row_at(k, needed):
         source = lax.rem(z + k, NZD)
-        remote(e2.at[source], e2.at[source], sd2.at[0], rd2.at[source], me).wait_recv()
-
-    @pl.when(z > 0)
-    def _():
-        for k in range(1, NZD):
-            from_row_of(k)
-
-    @pl.when(z == 0)
-    def _():
-        from_row_of(last_z)
-
+        uses = (source < z) | (source == last_z)
+
+        @pl.when(uses if needed else jnp.logical_not(uses))
+        def _():
+            remote(e2.at[source], e2.at[source], sd2.at[0], rd2.at[source], me).wait_recv()
+
+    for k in range(1, NZD):
+        from_row_at(k, True)
     carry[0:per] = e2[last_z, per : 2 * per]
-
-    @pl.when(z > 0)
-    def _():
-        arrive = carry[0:per]
-        for s in range(NZD - 1):
-            passed_on = e2[s, 0:per] * arrive + e2[s, per : 2 * per]
-            arrive = jnp.where(s < z, passed_on, arrive)
-        carry[0:per] = arrive
+    for s in range(NZD - 1):
+
+        @pl.when(s < z)
+        def _():
+            carry[0:per] = e2[s, 0:per] * carry[0:per] + e2[s, per : 2 * per]
 
     arrive = carry[0:per]
     for i in range(NXD):
@@ -544,25 +542,25 @@
     edges[0] = GAIN * (ROOT * from_low + halo[0, 0, 0] * (kappa_along + half * fbuf[0, 0]))
     edges[1] = GAIN * (ROOT * from_high + halo[1, 0, 0] * (kappa_along - half * fbuf[0, XL - 1]))
 
-    @pl.when(z == 0)
-    def _():
-        for k in range(1, last_z):
-            from_row_of(k)
-        for far in FAR:
+    for k in range(1, NZD):
+        from_row_at(k, False)
+
+    @pl.when(z < FIRST)
+    def _():
+        for i, far in enumerate(FAR):
             arrived(far)
             for k in (1, 2, 3):
                 source = lax.rem(x + k, NXD)
-                remote(r4.at[far - FAR[0], source], r4.at[far - FAR[0], source], ss4.at[0], rs4.at[far - FAR[0], source], me).wait_recv()
-            r4[far - FAR[0], x] = r2[far]
+                remote(r4.at[i, source], r4.at[i, source], ss4.at[0, 0], rs4.at[i, source], me).wait_recv()
+            r4[i, x] = r2[lax.rem(z + far, NZD)]
         along = pick([power(XL * i) for i in range(NXD)], x)
         against = pick([power(XL * (NXD - 1 - i)) for i in range(NXD)], x)
         for q in range(NXD):
             part = slice(q * quarter, (q + 1) * quarter)
-            up_sum = from_above_f(0, FAR[0]) * r4[0, q]
-            down_sum = from_above_b(0, FAR[0]) * r4[0, q]
-            for far in FAR[1:]:
-                up_sum = up_sum + from_above_f(0, far) * r4[far - FAR[0], q]
-                down_sum = down_sum + from_above_b(0, far) * r4[far - FAR[0], q]
+            up_sum, down_sum = jnp.zeros((quarter, 128), jnp.float32), jnp.zeros((quarter, 128), jnp.float32)
+            for i, far in enumerate(FAR):
+                up_sum = up_sum + pick([from_above_f(t, t + far) for t in range(FIRST)], z) * r4[i, q]
+                down_sum = down_sum + pick([from_above_b(t, t + far) for t in range(FIRST)], z) * r4[i, q]
             edges[0, part] = edges[0, part] + (GAIN * ROOT) * along * up_sum
             edges[1, part] = edges[1, part] + (GAIN * ROOT) * against * down_sum
 
@@ -574,10 +572,12 @@
     for copy in sends:
         copy.wait_send()
 
-    @pl.when(is_far)
-    def _():
-        for copy in to_first():
-            copy.wait_send()
+    for t, i in far_pairs:
+
+        @pl.when(z == t + FAR[i])
+        def _():
+            for copy in to_first(t, i):
+                copy.wait_send()
 
     @pl.when((x == 0) & (z > 0))
     def _():
@@ -690,7 +690,7 @@
             dma((NZD,)),
             dma((NXD - 1,)),
             dma((NXD,)),
-            dma((NXD - 1,)),
+            dma((len(FAR), NXD - 1)),
             dma((len(FAR), NXD)),
             dma((NXD - 1,)),
             dma((NXD,)),

time: 24.4 us -> 24.3 us (level)
  no operation moved by 1% of the time
where the time goes in v3:
time: 24.3 us; the launch traced here: 24.2 us
  Pallas kernels  23.6 us (97%)
  between operations  0.64 us (3%)
    pallas_call x1, Pallas kernels, body(): pl.pallas_call(tunnel_kernel, out_shape=tuple((jax.ShapeDtypeStruct(shape...  20.9 us
    pallas_call x1, Pallas kernels, body(): pl.pallas_call(write_kernel, out_shape=(jax.ShapeDtypeStruct(fields.shape...  2.69 us

profile of v3, /device:TPU:8, one launch (start us, length us, event | category | flops | bytes accessed | tf_op | source)
XLA Modules:
  0.0 24.2 jit_solution(14789529167126171373)
XLA Ops:
  0.6 20.9 %tunnel_step.1 = (f32[5,32,64,128]{3,2,1,0:T(8,128)S(1)}, f32[2,64,128]{2,1,0:T(8,128)S(1)}, f32[3,4,128,128]{3,2,1,0:T(8,128)S(1)}, f32[12,8,128]{2,1,0:T(8,128...) custom-call(f32[5,32,64,128]{3,2,1,0:T(8,128)} %fields.1, f32[3,128,512]{2,1,0:T(8,128)} %down.1, s32[4]{0:T(128)} %fire_x.1, ...), custom_call_target="tpu_custom_call" | custom-call | tf_op jit(solution)/shard_map/tunnel_step/pallas_call | solution.py:646
  21.5 2.7 %write_out.1 = (f32[5,32,64,128]{3,2,1,0:T(8,128)}, f32[3,128,512]{2,1,0:T(8,128)}) custom-call(f32[5,32,64,128]{3,2,1,0:T(8,128)S(1)} %get-tuple-element.8.near_in, f32[2,64,128]{2,1,0:T(8,128)S(1)} %get-tuple-element.9.edges, f32[3,4,128,128]{3,2,1,0:T(8,128)S(1)} %get-tuple-element.10.dbuf, f32[12,8,128]{2,1,0:T(8,128)S(1)} %get-tuple-element.11.fac, ...), custom_call_target="tpu_custom_call" | custom-call | tf_op jit(solution)/shard_map/write_out/pallas_call | solution.py:707
